TPU v7x, 32 devices: a whole 2x2x4 slice. The times are simulated.
32 devices in a mesh: ctx: 8 (over y, x, core), fsdp: 4 (over z).
Axes of the slice: x: 2, y: 2, z: 4, core: 2. Of those that a mesh axis runs over, the one named last changes fastest.
Arguments:
- tokens: bfloat16 [4, 4096, 768], P('fsdp', 'ctx'), may hold values from -6 to 6
- cotangent: bfloat16 [4, 4096, 768], P('fsdp', 'ctx'), may hold values from -6 to 6
- lengths: int32 [4, 4], P('fsdp'), may hold values from 1 to 2048, 4096 in all within a row
- dealing: int32 [4, 16], P('fsdp'), may hold values from 0 to 15, each once within a row
- qkv_weight: bfloat16 [768, 2304], P('fsdp'), may hold values from -0.21875 to 0.21875
- out_weight: bfloat16 [768, 768], P('fsdp'), may hold values from -0.21875 to 0.21875
- in_weight: bfloat16 [768, 3072], P('fsdp'), may hold values from -0.21875 to 0.21875
- back_weight: bfloat16 [3072, 768], P('fsdp'), may hold values from -0.109375 to 0.109375
- norm_gains: bfloat16 [3, 768], P(None, 'fsdp'), may hold values from 0.25 to 1.75
- shifts: bfloat16 [7, 768], P(None, 'fsdp'), may hold values from -1.796875 to 1.796875
- ffn_gain: bfloat16 [3072], P('fsdp'), may hold values from 0.25 to 1.75
- ffn_shifts: bfloat16 [2, 3072], P(None, 'fsdp'), may hold values from -1.796875 to 1.796875
Outputs:
- mixed_out: bfloat16 [4, 4096, 768], P('fsdp', 'ctx')
- input_grad: float32 [4, 4096, 768], P('fsdp', 'ctx')
- qkv_grad: float32 [768, 2304], P(('ctx', 'fsdp'))
- out_grad: float32 [768, 768], P(('ctx', 'fsdp'))
- in_grad: float32 [768, 3072], P(('ctx', 'fsdp'))
- back_grad: float32 [3072, 768], P(('ctx', 'fsdp'))
- gains_grad: float32 [3, 768], P(None, ('ctx', 'fsdp'))
- shifts_grad: float32 [7, 768], P(None, ('ctx', 'fsdp'))
- ffn_gain_grad: float32 [3072], P(('ctx', 'fsdp'))
- ffn_shifts_grad: float32 [2, 3072], P(None, ('ctx', 'fsdp'))
Inputs may be any that keep to these rules, and one draw needn't show every extreme that they name: `lengths`: each row sums to 4096 and its largest entry is exactly 2048. `dealing`: each row is a permutation of the group numbers.
All inputs are finite; a program needn't handle non-finite values.
Results may differ from a plain program's by a relative error of at most 0.018.
Values may be sent and summed in bfloat16 or wider, within the bound.
No kernel may reach another device: no remote copies, remote signals or barrier semaphores. Data moves between devices by JAX's collectives and lax.ppermute only.
A program may use at most 256 MiB of HBM per device.

v0:
```python
import math
import jax
import jax.numpy as jnp
from jax import lax
from jax.sharding import PartitionSpec as P

D = 768
H = 12
DH = 64


def layer_norm(values, gain, shift):
    average = jnp.mean(values, axis=-1, keepdims=True)
    centred = values - average
    variance = jnp.mean(centred * centred, axis=-1, keepdims=True)
    return centred * lax.rsqrt(variance + 1e-05) * gain + shift


def gelu_exact(values):
    return jax.nn.gelu(values, approximate=False)


def row_places(first_row, row_count, deal_row, bounds, group_rows):
    row_ids = first_row + jnp.arange(row_count, dtype=jnp.int32)
    group_ids = row_ids // group_rows
    onehot = (group_ids[:, None] == jnp.arange(deal_row.shape[0], dtype=jnp.int32)[None, :]).astype(
        jnp.int32
    )
    picked = jnp.sum(onehot * deal_row[None, :], axis=1)
    places = picked * group_rows + row_ids % group_rows
    segment = jnp.sum((places[:, None] >= bounds[None, :]).astype(jnp.int32), axis=1)
    return (places, segment)


def outer_sum(left, right):
    return lax.dot_general(
        left, right, (((0,), (0,)), ((), ())), preferred_element_type=jnp.float32
    )


def times_transposed(left, matrix):
    return lax.dot_general(
        left, matrix, (((1,), (1,)), ((), ())), preferred_element_type=jnp.float32
    )


def unpack(loaded):
    qkv_w, out_w, in_w, back_w, gains, shift_rows, ffn_gain, ffn_shift_rows = loaded
    return (
        qkv_w,
        out_w,
        in_w,
        back_w,
        gains.astype(jnp.float32),
        shift_rows.astype(jnp.float32),
        ffn_gain.astype(jnp.float32),
        ffn_shift_rows.astype(jnp.float32),
    )


def local(
    tokens,
    cotangent,
    lengths,
    dealing,
    qkv_weight,
    out_weight,
    in_weight,
    back_weight,
    norm_gains,
    shifts,
    ffn_gain,
    ffn_shifts,
):
    position = lax.axis_index("ctx")
    tok_rows = tokens.shape[1]
    group_rows = tok_rows // 2
    deal_row = dealing[0]
    bounds = jnp.cumsum(lengths[0])
    scaling = DH ** (-0.5)
    loaded = (
        lax.all_gather(qkv_weight, "fsdp", axis=0, tiled=True),
        lax.all_gather(out_weight, "fsdp", axis=0, tiled=True),
        lax.all_gather(in_weight, "fsdp", axis=0, tiled=True),
        lax.all_gather(back_weight, "fsdp", axis=0, tiled=True),
        lax.all_gather(norm_gains, "fsdp", axis=1, tiled=True),
        lax.all_gather(shifts, "fsdp", axis=1, tiled=True),
        lax.all_gather(ffn_gain, "fsdp", axis=0, tiled=True),
        lax.all_gather(ffn_shifts, "fsdp", axis=1, tiled=True),
    )
    qkv_w, out_w, in_w, back_w, gains, shift_rows, ffn_scale, ffn_shift_rows = unpack(loaded)
    inputs = tokens[0].astype(jnp.float32)
    normed = layer_norm(inputs, gains[0], shift_rows[0])
    normed_low = normed.astype(jnp.bfloat16)
    projected = jnp.dot(normed_low, qkv_w, preferred_element_type=jnp.float32)
    query = (projected[:, :D] + shift_rows[1]).astype(jnp.bfloat16)
    keyed = projected[:, D : 2 * D].astype(jnp.bfloat16)
    valued = (projected[:, 2 * D :] + shift_rows[2]).astype(jnp.bfloat16)
    query3 = query.reshape(tok_rows, H, DH)
    q_places, q_segment = row_places(position * tok_rows, tok_rows, deal_row, bounds, group_rows)

    def allowed_pairs(qp, qs, k_places, k_segment):
        return ((k_segment[None, :] == qs[:, None]) & (k_places[None, :] <= qp[:, None]))[None]

    initial = (
        jnp.full((H, tok_rows), -1e30, jnp.float32),
        jnp.zeros((H, tok_rows), jnp.float32),
        jnp.zeros((H, tok_rows, DH), jnp.float32),
    )
    key_rows = lax.all_gather(keyed, "ctx", axis=0, tiled=True)
    value_rows = lax.all_gather(valued, "ctx", axis=0, tiled=True)
    key_count = key_rows.shape[0]
    block_rows = 512
    block_count = key_count // block_rows
    k_places, k_segment = row_places(jnp.int32(0), key_count, deal_row, bounds, group_rows)
    stacked = (
        key_rows.reshape(block_count, block_rows, H, DH),
        value_rows.reshape(block_count, block_rows, H, DH),
        k_places.reshape(block_count, block_rows),
        k_segment.reshape(block_count, block_rows),
    )

    def visit_block(inner_state, pieces):
        maxima, totals, weighted = inner_state
        key3, value3, block_places, block_segment = pieces
        scores = (
            jnp.einsum("qhd,khd->hqk", query3, key3, preferred_element_type=jnp.float32) * scaling
        )
        allowed = allowed_pairs(q_places, q_segment, block_places, block_segment)
        masked = jnp.where(allowed, scores, -1e30)
        raised = jnp.maximum(maxima, jnp.max(masked, axis=-1))
        rescale = jnp.exp(maxima - raised)
        expo = jnp.where(allowed, jnp.exp(masked - raised[..., None]), 0.0)
        totals = totals * rescale + jnp.sum(expo, axis=-1)
        weighted = weighted * rescale[..., None] + jnp.einsum(
            "hqk,khd->hqd", expo.astype(jnp.bfloat16), value3, preferred_element_type=jnp.float32
        )
        return ((raised, totals, weighted), None)

    maxima, totals, weighted = lax.scan(visit_block, initial, stacked)[0]
    context3 = weighted / totals[..., None]
    log_total = maxima + jnp.log(totals)
    context = context3.transpose(1, 0, 2).reshape(tok_rows, D)
    inner = layer_norm(context, gains[1], shift_rows[3])
    inner_low = inner.astype(jnp.bfloat16)
    branch = jnp.dot(inner_low, out_w, preferred_element_type=jnp.float32) + shift_rows[4]
    middle = inputs + branch
    normed_two = layer_norm(middle, gains[2], shift_rows[5])
    normed_two_low = normed_two.astype(jnp.bfloat16)
    hidden = jnp.dot(normed_two_low, in_w, preferred_element_type=jnp.float32) + ffn_shift_rows[0]
    activated = gelu_exact(hidden)
    inner_two = layer_norm(activated, ffn_scale, ffn_shift_rows[1])
    inner_two_low = inner_two.astype(jnp.bfloat16)
    result = jnp.dot(inner_two_low, back_w, preferred_element_type=jnp.float32) + shift_rows[6]
    mixed_out = (middle + result).astype(jnp.bfloat16)
    loaded_back = (
        lax.all_gather(qkv_weight, "fsdp", axis=0, tiled=True),
        lax.all_gather(out_weight, "fsdp", axis=0, tiled=True),
        lax.all_gather(in_weight, "fsdp", axis=0, tiled=True),
        lax.all_gather(back_weight, "fsdp", axis=0, tiled=True),
        lax.all_gather(norm_gains, "fsdp", axis=1, tiled=True),
        lax.all_gather(shifts, "fsdp", axis=1, tiled=True),
        lax.all_gather(ffn_gain, "fsdp", axis=0, tiled=True),
        lax.all_gather(ffn_shifts, "fsdp", axis=1, tiled=True),
    )
    qkv_w, out_w, in_w, back_w, gains, shift_rows, ffn_scale, ffn_shift_rows = unpack(loaded_back)
    upstream = cotangent[0].astype(jnp.float32)
    result_low = cotangent[0]
    grad_back_w = outer_sum(inner_two_low, result_low)
    grad_back_bias = jnp.sum(result_low.astype(jnp.float32), axis=0)
    grad_inner_two = times_transposed(result_low, back_w)
    norm_pull = jax.vjp(layer_norm, activated, ffn_scale, ffn_shift_rows[1])[1]
    grad_activated, grad_ffn_gain, grad_ffn_shift = norm_pull(grad_inner_two)
    gelu_pull = jax.vjp(gelu_exact, hidden)[1]
    grad_hidden = gelu_pull(grad_activated)[0]
    hidden_low = grad_hidden.astype(jnp.bfloat16)
    grad_in_w = outer_sum(normed_two_low, hidden_low)
    grad_in_bias = jnp.sum(hidden_low.astype(jnp.float32), axis=0)
    grad_normed_two = times_transposed(hidden_low, in_w)
    second_pull = jax.vjp(layer_norm, middle, gains[2], shift_rows[5])[1]
    grad_middle_part, grad_gain_two, grad_shift_five = second_pull(grad_normed_two)
    grad_middle = upstream + grad_middle_part
    branch_low = grad_middle.astype(jnp.bfloat16)
    grad_out_w = outer_sum(inner_low, branch_low)
    grad_out_bias = jnp.sum(branch_low.astype(jnp.float32), axis=0)
    grad_inner = times_transposed(branch_low, out_w)
    inner_pull = jax.vjp(layer_norm, context, gains[1], shift_rows[3])[1]
    grad_context, grad_gain_one, grad_shift_three = inner_pull(grad_inner)
    context_grad_low = grad_context.astype(jnp.bfloat16).reshape(tok_rows, H, DH)
    delta = jnp.einsum("qhd,hqd->hq", context_grad_low.astype(jnp.float32), context3)

    def grad_pair(
        q_rows, grad_rows, lse_rows, delta_rows, qp, qs, key3, value3, k_places, k_segment
    ):
        scores = (
            jnp.einsum("qhd,khd->hqk", q_rows, key3, preferred_element_type=jnp.float32) * scaling
        )
        allowed = allowed_pairs(qp, qs, k_places, k_segment)
        probabilities = jnp.where(allowed, jnp.exp(scores - lse_rows[..., None]), 0.0)
        upstream_probs = jnp.einsum(
            "qhd,khd->hqk", grad_rows, value3, preferred_element_type=jnp.float32
        )
        score_grad = (probabilities * (upstream_probs - delta_rows[..., None])).astype(jnp.bfloat16)
        query_add = (
            jnp.einsum("hqk,khd->qhd", score_grad, key3, preferred_element_type=jnp.float32)
            * scaling
        )
        key_add = (
            jnp.einsum("hqk,qhd->khd", score_grad, q_rows, preferred_element_type=jnp.float32)
            * scaling
        )
        value_add = jnp.einsum(
            "hqk,qhd->khd",
            probabilities.astype(jnp.bfloat16),
            grad_rows,
            preferred_element_type=jnp.float32,
        )
        return (query_add, key_add, value_add)

    def grad_block(key3, value3, k_places, k_segment):
        return grad_pair(
            query3,
            context_grad_low,
            log_total,
            delta,
            q_places,
            q_segment,
            key3,
            value3,
            k_places,
            k_segment,
        )

    zero_query = jnp.zeros((tok_rows, H, DH), jnp.float32)
    gathered_keys, gathered_values = (
        lax.all_gather(keyed, "ctx", axis=0, tiled=True),
        lax.all_gather(valued, "ctx", axis=0, tiled=True),
    )
    stream_rows = gathered_keys.shape[0]
    block_rows = math.gcd(stream_rows, 512)
    block_count = stream_rows // block_rows
    all_places, all_segment = row_places(0, stream_rows, deal_row, bounds, group_rows)

    def sweep(query_grad, pieces):
        key3, value3, block_places, block_segment = pieces
        query_add, key_add, value_add = grad_block(key3, value3, block_places, block_segment)
        return (query_grad + query_add, (key_add, value_add))

    query_grad, (key_parts, value_parts) = lax.scan(
        sweep,
        zero_query,
        (
            gathered_keys.reshape(block_count, block_rows, H, DH),
            gathered_values.reshape(block_count, block_rows, H, DH),
            all_places.reshape(block_count, block_rows),
            all_segment.reshape(block_count, block_rows),
        ),
    )
    key_terms = key_parts.reshape(stream_rows, D)
    value_terms = value_parts.reshape(stream_rows, D)
    key_grad_mine, value_grad_mine = (
        lax.psum_scatter(
            key_terms.astype(jnp.bfloat16), "ctx", scatter_dimension=0, tiled=True
        ).astype(jnp.float32),
        lax.psum_scatter(
            value_terms.astype(jnp.bfloat16), "ctx", scatter_dimension=0, tiled=True
        ).astype(jnp.float32),
    )
    qkv_grad_low = jnp.concatenate(
        [query_grad.reshape(tok_rows, D), key_grad_mine, value_grad_mine], axis=1
    ).astype(jnp.bfloat16)
    grad_qkv_w = outer_sum(normed_low, qkv_grad_low)
    column_sums = jnp.sum(qkv_grad_low.astype(jnp.float32), axis=0)
    grad_query_bias = column_sums[:D]
    grad_value_bias = column_sums[2 * D :]
    grad_normed = times_transposed(qkv_grad_low, qkv_w)
    first_pull = jax.vjp(layer_norm, inputs, gains[0], shift_rows[0])[1]
    grad_inputs_part, grad_gain_zero, grad_shift_zero = first_pull(grad_normed)
    input_grad = grad_middle + grad_inputs_part
    gains_terms = jnp.stack([grad_gain_zero, grad_gain_one, grad_gain_two])
    shift_terms = jnp.stack(
        [
            grad_shift_zero,
            grad_query_bias,
            grad_value_bias,
            grad_shift_three,
            grad_out_bias,
            grad_shift_five,
            grad_back_bias,
        ]
    )
    ffn_shift_terms = jnp.stack([grad_in_bias, grad_ffn_shift])
    reduced = (
        lax.psum_scatter(grad_qkv_w, ("ctx", "fsdp"), scatter_dimension=0, tiled=True),
        lax.psum_scatter(grad_out_w, ("ctx", "fsdp"), scatter_dimension=0, tiled=True),
        lax.psum_scatter(grad_in_w, ("ctx", "fsdp"), scatter_dimension=0, tiled=True),
        lax.psum_scatter(grad_back_w, ("ctx", "fsdp"), scatter_dimension=0, tiled=True),
        lax.psum_scatter(gains_terms, ("ctx", "fsdp"), scatter_dimension=1, tiled=True),
        lax.psum_scatter(shift_terms, ("ctx", "fsdp"), scatter_dimension=1, tiled=True),
        lax.psum_scatter(grad_ffn_gain, ("ctx", "fsdp"), scatter_dimension=0, tiled=True),
        lax.psum_scatter(ffn_shift_terms, ("ctx", "fsdp"), scatter_dimension=1, tiled=True),
    )
    return (mixed_out[None], input_grad[None]) + tuple(reduced)


def solution(mesh):
    in_specs = (
        P("fsdp", "ctx", None),
        P("fsdp", "ctx", None),
        P("fsdp", None),
        P("fsdp", None),
        P("fsdp", None),
        P("fsdp", None),
        P("fsdp", None),
        P("fsdp", None),
        P(None, "fsdp"),
        P(None, "fsdp"),
        P("fsdp"),
        P(None, "fsdp"),
    )
    out_specs = (
        P("fsdp", "ctx", None),
        P("fsdp", "ctx", None),
        P(("ctx", "fsdp"), None),
        P(("ctx", "fsdp"), None),
        P(("ctx", "fsdp"), None),
        P(("ctx", "fsdp"), None),
        P(None, ("ctx", "fsdp")),
        P(None, ("ctx", "fsdp")),
        P(("ctx", "fsdp")),
        P(None, ("ctx", "fsdp")),
    )
    return jax.shard_map(local, mesh=mesh, in_specs=in_specs, out_specs=out_specs, check_vma=False)
```

profile of v0, /device:TPU:0, one launch (start us, length us, event | category | flops | bytes accessed | tf_op | source)
XLA Modules:
  0.0 1461.5 jit_solution(8794208688010352200)
XLA Ops:
  8.0 14.9 %all-gather.1 = bf16[4,192,7]{1,2,0:T(8,128)(2,1)S(1)} all-gather(bf16[1,192,7]{1,2,0:T(8,128)(2,1)} %bitcast.267), channel_id=1, replica_groups=mesh['ctx'=8,'fsdp'=4] {'fsdp'}, dimensions={0}, use_global_device_ids=true | all-gather | bytes 13440 | tf_op jit(solution)/shard_map/all_gather | solution.py:87
  23.0 12.2 all-gather
  38.9 43.6 %all-gather.10.cloned.1.call-done = bf16[768,2304]{1,0:T(8,128)(2,1)} async-done(((bf16[192,2304]{1,0:T(8,128)(2,1)}), bf16[768,2304]{1,0:T(8,128)(2,1)}) %all-gather.10.cloned.1.call-update) | async-done | bytes 3538960 | tf_op jit(solution)/shard_map/all_gather | solution.py:82
  95.8 13.0 all_gather.45
  109.5 13.6 all-gather.2
  124.2 10.1 all-gather.12.cloned.1.call-done
  134.3 8.6 copy.91
  142.9 7.5 copy.120
  155.3 26.5 %all-gather.14.cloned.1.call-done = bf16[4096,768]{1,0:T(8,128)(2,1)} async-done(((bf16[512,768]{1,0:T(8,128)(2,1)}), bf16[4096,768]{1,0:T(8,128)(2,1)}) %all-gather.14.cloned.1.call-update) | async-done | bytes 6291472 | tf_op jit(solution)/shard_map/all_gather | solution.py:111
  181.8 8.9 copy.93
  202.6 179.3 %while.30 = (s32[]{:T(128)}, f32[12,512]{1,0:T(8,128)S(1)}, f32[12,512]{1,0:T(8,128)S(1)}, f32[12,512,64]{1,2,0:T(8,128)}, s32[8,512]{1,0:T(8,128)S(1)}, /*index...) while((s32[]{:T(128)}, f32[12,512]{1,0:T(8,128)S(1)}, ...), condition=%wide.region_10.11_spmd.clone, body=%wide.region_7.10_spmd.clone.sunk | while | flops 848197632 | bytes 95043760 | solution.py:140
  202.9 8.0 fusion.150
  210.9 7.7 fusion.151
  225.0 8.0 fusion.150
  233.0 7.7 fusion.151
  247.4 8.0 fusion.150
  255.5 7.7 fusion.151
  269.9 8.0 fusion.150
  277.9 7.6 fusion.151
  292.3 8.0 fusion.150
  300.3 7.7 fusion.151
  314.7 8.0 fusion.150
  322.7 7.7 fusion.151
  337.1 8.0 fusion.150
  345.2 7.7 fusion.151
  359.6 8.0 fusion.150
  367.6 7.6 fusion.151
  389.9 21.5 %fusion.101 = (f32[512]{0:T(512)S(1)}, f32[512,3072]{1,0:T(8,128)}, f32[512,3072]{1,0:T(8,128)}, f32[512,3072]{1,0:T(8,128)}) fusion(f32[3072]{0:T(1024)S(1)} %bitcast.261, bf16[768,3072]{1,0:T(8,128)(2,1)} %all-gather.18.cloned.1.call-done, f32[512,768]{1,0:T(8,128)} %copy-done.10, f32[768]{0:T(1024)S(1)} %get-tuple-element.371, ...), kind=kOutput, calls=%fused_computation.205 | convolution fusion | flops 2521693696 | bytes 25190400 | tf_op jit(solution)/shard_map/dot_general | solution.py:150
  411.4 7.4 multiply_reduce_fusion.1
  422.2 10.8 convert_reduce_fusion
  447.7 251.0 %while.31 = (s32[]{:T(128)}, f32[512,12,64]{0,2,1:T(8,128)}, bf16[8,512,12,64]{1,3,2,0:T(8,128)(2,1)}, bf16[8,512,12,64]{1,3,2,0:T(8,128)(2,1)}, bf16[8,512,12,6...) while((s32[]{:T(128)}, f32[512,12,64]{0,2,1:T(8,128)}, ...), condition=%wide.region_24.25_spmd.clone, body=%wide.region_23.24_spmd.clone.sunk | while | flops 2047082496 | bytes 195125520 | solution.py:249
  455.7 8.4 fusion.165
  486.7 8.4 fusion.165
  518.1 8.4 fusion.165
  549.4 8.4 fusion.165
  580.8 8.4 fusion.165
  612.1 8.4 fusion.165
  643.5 8.4 fusion.165
  674.9 8.4 fusion.165
  733.2 7.2 fusion.95
  750.1 24.5 %reduce-scatter.14.cloned.1.call-done = bf16[512,768]{0,1:T(8,128)(2,1)} async-done(((bf16[4096,768]{0,1:T(8,128)(2,1)}), bf16[512,768]{0,1:T(8,128)(2,1)}) %reduce-scatter.14.cloned.1.call-update) | async-done | bytes 786448 | tf_op jit(solution)/shard_map/reduce_scatter | solution.py:265
  774.6 65.5 %reduce-scatter.12.cloned.1.call-done = bf16[512,768]{0,1:T(8,128)(2,1)} async-done(((bf16[4096,768]{0,1:T(8,128)(2,1)}), bf16[512,768]{0,1:T(8,128)(2,1)}) %reduce-scatter.12.cloned.1.call-update) | async-done | bytes 786448 | tf_op jit(solution)/shard_map/reduce_scatter | solution.py:262
  855.0 87.4 %reduce-scatter.24.cloned.1.call-done = f32[96,2]{1,0:T(8,128)} async-done(((f32[3072,2]{1,0:T(8,128)}), f32[96,2]{1,0:T(8,128)}) %reduce-scatter.24.cloned.1.call-update) | async-done | bytes 784
  952.3 40.7 %all-reduce.3 = (f32[3,768]{1,0:T(4,128)S(1)}, f32[7,768]{1,0:T(8,128)S(1)}, f32[3072]{0:T(1024)S(1)}) all-reduce(f32[3,768]{1,0:T(4,128)S(1)} %pad_maximum_fusion.2, f32[7,768]{1,0:T(8,128)S(1)} %stack.36, f32[3072]{0:T(1024)S(1)} %copy-done.25), channel_id=8, replica_groups=mesh['ctx'=8,'fsdp'=4] {'ctx','fsdp'}, use_global_device_ids=true, to_apply=%region_36.37.clone | all-reduce | flops 10752 | bytes 86016
  994.9 51.3 %reduce-scatter.18.cloned.1.call-done = f32[24,768]{1,0:T(8,128)} async-done(((f32[768,768]{1,0:T(8,128)}), f32[24,768]{1,0:T(8,128)}) %reduce-scatter.18.cloned.1.call-update) | async-done | bytes 73744 | tf_op jit(solution)/shard_map/reduce_scatter | solution.py:295
  1046.2 142.2 %reduce-scatter.20.cloned.1.call-done = f32[24,3072]{1,0:T(8,128)} async-done(((f32[768,3072]{1,0:T(8,128)}), f32[24,3072]{1,0:T(8,128)}) %reduce-scatter.20.cloned.1.call-update) | async-done | bytes 294928 | tf_op jit(solution)/shard_map/reduce_scatter | solution.py:296
  1188.4 140.8 %reduce-scatter.22.cloned.1.call-done = f32[96,768]{1,0:T(8,128)} async-done(((f32[3072,768]{1,0:T(8,128)}), f32[96,768]{1,0:T(8,128)}) %reduce-scatter.22.cloned.1.call-update) | async-done | bytes 294928 | tf_op jit(solution)/shard_map/reduce_scatter | solution.py:297
  1329.2 125.6 %reduce-scatter.16.cloned.1.call-done = f32[24,2304]{1,0:T(8,128)} async-done(((f32[768,2304]{1,0:T(8,128)}), f32[24,2304]{1,0:T(8,128)}) %reduce-scatter.16.cloned.1.call-update) | async-done | bytes 221200 | tf_op jit(solution)/shard_map/reduce_scatter | solution.py:294
  (387 shorter events, 368.8 us)
Async XLA Ops:
  7.2 75.3 %all-gather.10.cloned.1.call-start = ((), (), s32[]{:S(2)}) async-start(), calls=%async_computation.7 | async-start | bytes 4423680 | tf_op jit(solution)/shard_map/all_gather | solution.py:82
  7.9 126.4 %all-gather.12.cloned.1.call-start = ((), (), s32[]{:S(2)}) async-start(), calls=%async_computation.8 | async-start | bytes 7077888 | tf_op jit(solution)/shard_map/all_gather | solution.py:110
  35.4 51.5 %copy-start.26 = (f32[768]{0:T(1024)}, f32[768]{0:T(1024)S(1)}, u32[]{:S(2)}) copy-start(f32[768]{0:T(1024)S(1)} %get-tuple-element.379) | copy-start | bytes 9220
  36.0 50.9 %copy-start.39 = (f32[768]{0:T(1024)}, f32[768]{0:T(1024)S(1)}, u32[]{:S(2)}) copy-start(f32[768]{0:T(1024)S(1)} %get-tuple-element.376) | copy-start | bytes 9220
  36.0 349.6 %copy-start.43 = (f32[768]{0:T(1024)}, f32[768]{0:T(1024)S(1)}, u32[]{:S(2)}) copy-start(f32[768]{0:T(1024)S(1)} %get-tuple-element.373) | copy-start | bytes 9220
  36.0 353.9 %copy-start.41 = (f32[768]{0:T(1024)}, f32[768]{0:T(1024)S(1)}, u32[]{:S(2)}) copy-start(f32[768]{0:T(1024)S(1)} %get-tuple-element.371) | copy-start | bytes 9220
  37.3 49.5 %copy-start.28 = (f32[512]{0:T(512)}, f32[512]{0:T(512)S(1)}, u32[]{:S(2)}) copy-start(f32[512]{0:T(512)S(1)} %broadcast_multiply_fusion.4) | copy-start | bytes 6148
  38.8 48.0 %copy-start.32 = (f32[512]{0:T(512)}, f32[512]{0:T(512)S(1)}, u32[]{:S(2)}) copy-start(f32[512]{0:T(512)S(1)} %fusion.57) | copy-start | bytes 6148
  38.8 48.0 %copy-start.30 = (f32[512]{0:T(512)}, f32[512]{0:T(512)S(1)}, u32[]{:S(2)}) copy-start(f32[512]{0:T(512)S(1)} %fusion.83) | copy-start | bytes 6148
  90.1 19.4 %copy-start.51 = (bf16[768]{0:T(1024)(128)(2,1)S(1)}, bf16[768]{0:T(1024)(128)(2,1)}, u32[]{:S(2)}) copy-start(bf16[768]{0:T(1024)(128)(2,1)} %param.26) | copy-start | bytes 4612
  90.1 91.7 %all-gather.14.cloned.1.call-start = ((), (), s32[]{:S(2)}) async-start(), calls=%async_computation.9 | async-start | bytes 7077888 | tf_op jit(solution)/shard_map/all_gather | solution.py:111
  93.2 292.3 %all-gather.16.cloned.1.call-start = ((), (), s32[]{:S(2)}) async-start(), calls=%async_computation.10 | async-start | bytes 1474560 | tf_op jit(solution)/shard_map/all_gather | solution.py:83
  93.8 296.1 %all-gather.18.cloned.1.call-start = ((), (), s32[]{:S(2)}) async-start(), calls=%async_computation.11 | async-start | bytes 5898240 | tf_op jit(solution)/shard_map/all_gather | solution.py:84
  94.4 317.0 %all-gather.20.cloned.1.call-start = ((), (), s32[]{:S(2)}) async-start(), calls=%async_computation.12 | async-start | bytes 5898240 | tf_op jit(solution)/shard_map/all_gather | solution.py:85
  94.9 679.7 %reduce-scatter.14.cloned.1.call-start = ((), (), s32[]{:S(2)}) async-start(), calls=%async_computation.14 | async-start | bytes 7077888 | tf_op jit(solution)/shard_map/reduce_scatter | solution.py:265
  210.9 8.3 copy-start
  233.0 8.4 copy-start
  255.5 8.4 copy-start
  277.9 8.3 copy-start
  300.3 8.3 copy-start
  322.7 8.4 copy-start
  345.1 8.4 copy-start
  367.6 8.3 copy-start
  389.9 21.5 %copy-start.19 = (bf16[1,512,768]{2,1,0:T(8,128)(2,1)S(1)}, bf16[1,512,768]{2,1,0:T(8,128)(2,1)}, u32[]{:S(2)}) copy-start(bf16[1,512,768]{2,1,0:T(8,128)(2,1)} %param.17) | copy-start | bytes 2359300
  411.4 7.4 copy-start.5
  422.2 12.4 copy-start.11
  464.1 10.3 copy-start.3
  495.1 10.6 copy-start.3
  526.5 10.6 copy-start.3
  557.9 5.9 copy-start.1
  557.9 10.6 copy-start.3
  589.3 10.6 copy-start.3
  620.6 5.9 copy-start.1
  620.6 10.7 copy-start.3
  652.0 5.9 copy-start.1
  652.0 10.7 copy-start.3
  683.4 10.6 copy-start.3
  712.4 127.7 %reduce-scatter.12.cloned.1.call-start = ((), (), s32[]{:S(2)}) async-start(), calls=%async_computation.13 | async-start | bytes 7077888 | tf_op jit(solution)/shard_map/reduce_scatter | solution.py:262
  727.0 215.4 %reduce-scatter.24.cloned.1.call-start = ((), (), s32[]{:S(2)}) async-start(), calls=%async_computation.19 | async-start | bytes 1622016
  729.4 316.8 %reduce-scatter.18.cloned.1.call-start = ((), (), s32[]{:S(2)}) async-start(), calls=%async_computation.16 | async-start | bytes 2433024 | tf_op jit(solution)/shard_map/reduce_scatter | solution.py:295
  733.2 455.3 %reduce-scatter.20.cloned.1.call-start = ((), (), s32[]{:S(2)}) async-start(), calls=%async_computation.17 | async-start | bytes 9732096 | tf_op jit(solution)/shard_map/reduce_scatter | solution.py:296
  740.5 588.7 %reduce-scatter.22.cloned.1.call-start = ((), (), s32[]{:S(2)}) async-start(), calls=%async_computation.18 | async-start | bytes 9732096 | tf_op jit(solution)/shard_map/reduce_scatter | solution.py:297
  748.6 91.6 %copy-start.9 = (bf16[1,512,768]{2,1,0:T(8,128)(2,1)S(1)}, bf16[1,512,768]{2,1,0:T(8,128)(2,1)}, u32[]{:S(2)}) copy-start(bf16[1,512,768]{2,1,0:T(8,128)(2,1)} %param.16) | copy-start | bytes 2359300
  748.6 91.6 %copy-start.27 = (f32[768]{0:T(1024)S(1)}, f32[768]{0:T(1024)}, u32[]{:S(2)}) copy-start(f32[768]{0:T(1024)} %copy-done.26) | copy-start | bytes 9220
  748.6 91.6 %copy-start.29 = (f32[512]{0:T(512)S(1)}, f32[512]{0:T(512)}, u32[]{:S(2)}) copy-start(f32[512]{0:T(512)} %copy-done.28) | copy-start | bytes 6148
  748.6 91.6 %copy-start.31 = (f32[512]{0:T(512)S(1)}, f32[512]{0:T(512)}, u32[]{:S(2)}) copy-start(f32[512]{0:T(512)} %copy-done.30) | copy-start | bytes 6148
  748.6 91.6 %copy-start.40 = (f32[768]{0:T(1024)S(1)}, f32[768]{0:T(1024)}, u32[]{:S(2)}) copy-start(f32[768]{0:T(1024)} %copy-done.39) | copy-start | bytes 9220
  748.6 706.2 %reduce-scatter.16.cloned.1.call-start = ((), (), s32[]{:S(2)}) async-start(), calls=%async_computation.15 | async-start | bytes 7299072 | tf_op jit(solution)/shard_map/reduce_scatter | solution.py:294
  (47 other events, 153.6 us)
Sparse Core Ops, SparseCore 0:
  9.6 72.8 all-gather.9
  90.2 44.0 all-gather.11
  136.2 45.5 all-gather.13
  183.2 30.4 all-gather.15
  215.1 88.5 all-gather.17
  305.1 87.8 all-gather.19
  712.5 62.0 reduce-scatter.13
  778.4 61.7 reduce-scatter.11
  845.4 96.9 reduce-scatter.23
  948.1 98.0 reduce-scatter.17
  1053.7 134.6 reduce-scatter.19
  1194.8 134.4 reduce-scatter.21
  1336.4 118.3 reduce-scatter.15
where the time goes:
time: 1470 us; the launch traced here: 1460 us
  waiting for transfers between devices  720 us (49%)
  matrix products  403 us (27%)
  local copies, waits for them, and re-layouts  131 us (9%)
  other arithmetic  96.1 us (7%)
  blocking collectives  94.5 us (6%)
  between operations  14.9 us (1%)
    reduce_scatter x1, waiting for transfers between devices, local(): lax.psum_scatter(grad_in_w, ('ctx', 'fsdp'), scatter_dimension=0, tiled=T...  142 us
    reduce_scatter x1, waiting for transfers between devices, local(): lax.psum_scatter(grad_back_w, ('ctx', 'fsdp'), scatter_dimension=0, tiled...  141 us
    reduce_scatter x1, waiting for transfers between devices, local(): lax.psum_scatter(grad_qkv_w, ('ctx', 'fsdp'), scatter_dimension=0, tiled=...  126 us
    unnamed x14, waiting for transfers between devices  89.8 us
    dot_general x8, matrix products, grad_pair(): jnp.einsum('qhd,khd->hqk', grad_rows, value3, preferred_element_type=jnp....  67.5 us
    reduce_scatter x1, waiting for transfers between devices, local(): lax.psum_scatter(key_terms.astype(jnp.bfloat16), 'ctx', scatter_dimension...  65.5 us
    dot_general x8, matrix products, visit_block(): jnp.einsum('qhd,khd->hqk', query3, key3, preferred_element_type=jnp.float32)  64 us
    reduce_sum x8, other arithmetic, visit_block(): totals = totals * rescale + jnp.sum(expo, axis=-1)  61.3 us
  transfers between devices with their start and end apart: 13, of which 10 were waited for; matrix products, arithmetic and copies ran while one was open for 21% of the time, Pallas kernels for 0%

commit v1 on v0

--- a/solution.py
+++ b/solution.py
@@ -108,7 +108,12 @@
         jnp.zeros((H, tok_rows, DH), jnp.float32),
     )
     key_rows = lax.all_gather(keyed, "ctx", axis=0, tiled=True)
-    value_rows = lax.all_gather(valued, "ctx", axis=0, tiled=True)
+    ring = [valued]
+    for hop in range(7):
+        ring.append(lax.ppermute(ring[-1], "ctx", [(dev, (dev + 1) % 8) for dev in range(8)]))
+    value_rows = jnp.roll(
+        jnp.concatenate(ring[::-1], axis=0), (lax.axis_index("ctx") + 1) * ring[0].shape[0], axis=0
+    )
     key_count = key_rows.shape[0]
     block_rows = 512
     block_count = key_count // block_rows

time: 1470 us -> 1560 us (1.061)
  waiting for transfers between devices: 720 us -> 777 us
  local copies, waits for them, and re-layouts: 131 us -> 163 us
    ppermute x0 -> x7, waiting for transfers between devices: none -> 94.1 us  [local(): lax.ppermute(ring[-1], 'ctx', [(dev, (dev + 1) % 8) for dev in range(8)])]
    all_gather x1, waiting for transfers between devices: 26.5 us -> 0.02 us  [local(): lax.all_gather(valued, 'ctx', axis=0, tiled=True)]
    unnamed x112 -> x145, local copies, waits for them, and re-layouts: 54 us -> 73.4 us
  transfers between devices with their start and end apart: 13 -> 20, of which waited for: 10 -> 14; matrix products, arithmetic and copies ran while one was open for 21% -> 21% of each run, Pallas kernels for 0% -> 0%
where the time goes in v1:
time: 1560 us; the launch traced here: 1550 us
  waiting for transfers between devices  777 us (50%)
  matrix products  404 us (26%)
  local copies, waits for them, and re-layouts  163 us (10%)
  other arithmetic  96.3 us (6%)
  blocking collectives  94.6 us (6%)
    reduce_scatter x1, waiting for transfers between devices, local(): lax.psum_scatter(grad_in_w, ('ctx', 'fsdp'), scatter_dimension=0, tiled=T...  142 us
    reduce_scatter x1, waiting for transfers between devices, local(): lax.psum_scatter(grad_back_w, ('ctx', 'fsdp'), scatter_dimension=0, tiled...  141 us
    reduce_scatter x1, waiting for transfers between devices, local(): lax.psum_scatter(grad_qkv_w, ('ctx', 'fsdp'), scatter_dimension=0, tiled=...  125 us
    ppermute x7, waiting for transfers between devices, local(): lax.ppermute(ring[-1], 'ctx', [(dev, (dev + 1) % 8) for dev in range(8)])  94.1 us
    unnamed x14, waiting for transfers between devices  90 us
    unnamed x145, local copies, waits for them, and re-layouts  73.4 us
    dot_general x8, matrix products, grad_pair(): jnp.einsum('qhd,khd->hqk', grad_rows, value3, preferred_element_type=jnp....  67.5 us
    reduce_scatter x1, waiting for transfers between devices, local(): lax.psum_scatter(key_terms.astype(jnp.bfloat16), 'ctx', scatter_dimension...  65.5 us
  transfers between devices with their start and end apart: 20, of which 14 were waited for; matrix products, arithmetic and copies ran while one was open for 21% of the time, Pallas kernels for 0%

profile of v1, /device:TPU:0, one launch (start us, length us, event | category | flops | bytes accessed | tf_op | source)
XLA Modules:
  0.0 1552.9 jit_solution(1215625916999225624)
XLA Ops:
  8.0 14.9 all-gather.1
  23.0 12.2 all-gather
  38.9 43.6 %all-gather.10.cloned.1.call-done = bf16[768,2304]{1,0:T(8,128)(2,1)} async-done(((bf16[192,2304]{1,0:T(8,128)(2,1)}), bf16[768,2304]{1,0:T(8,128)(2,1)}) %all-gather.10.cloned.1.call-update) | async-done | bytes 3538960 | tf_op jit(solution)/shard_map/all_gather | solution.py:82
  94.3 20.7 %collective-permute-done = bf16[512,768]{1,0:T(8,128)(2,1)S(1)} collective-permute-done((bf16[512,768]{1,0:T(8,128)(2,1)S(1)}, bf16[512,768]{1,0:T(8,128)(2,1)S(1)}, u32[]{:S(2)}, u32[]{:S(2)}) %collective-permute-start) | collective-permute-done | bytes 786464 | tf_op jit(solution)/shard_map/ppermute | solution.py:113
  115.0 26.0 %collective-permute-done.1 = bf16[512,768]{1,0:T(8,128)(2,1)S(1)} collective-permute-done((bf16[512,768]{1,0:T(8,128)(2,1)S(1)}, bf16[512,768]{1,0:T(8,128)(2,1)S(1)}, u32[]{:S(2)}, u32[]{:S(2)}) %collective-permute-start.1) | collective-permute-done | bytes 786464 | tf_op jit(solution)/shard_map/ppermute | solution.py:113
  141.0 12.3 collective-permute-done.2
  153.3 12.4 collective-permute-done.3
  166.1 12.2 collective-permute-done.4
  178.5 13.2 all-gather.2
  192.4 13.3 all_gather.43
  208.0 10.5 collective-permute-done.6
  231.7 8.6 copy.95
  252.2 8.8 copy.93
  272.8 179.6 %while.30 = (s32[]{:T(128)}, f32[12,512]{1,0:T(8,128)S(1)}, f32[12,512]{1,0:T(8,128)S(1)}, f32[12,512,64]{1,2,0:T(8,128)}, s32[8,512]{1,0:T(8,128)S(1)}, /*index...) while((s32[]{:T(128)}, f32[12,512]{1,0:T(8,128)S(1)}, ...), condition=%wide.region_10.11_spmd.clone, body=%wide.region_7.10_spmd.clone.sunk | while | flops 848197632 | bytes 95043760 | solution.py:145
  273.1 8.2 fusion.150
  295.5 8.0 fusion.150
  303.5 7.7 fusion.151
  317.9 8.0 fusion.150
  340.4 8.0 fusion.150
  348.4 7.7 fusion.151
  362.7 8.1 fusion.150
  370.9 7.7 fusion.151
  385.2 8.0 fusion.150
  393.2 7.8 fusion.151
  407.7 8.0 fusion.150
  415.7 7.7 fusion.151
  430.0 8.0 fusion.150
  438.0 7.7 fusion.151
  460.4 21.6 %fusion.101 = (f32[512]{0:T(512)S(1)}, f32[512,3072]{1,0:T(8,128)}, f32[512,3072]{1,0:T(8,128)}, f32[512,3072]{1,0:T(8,128)}) fusion(f32[3072]{0:T(1024)S(1)} %bitcast.270, bf16[768,3072]{1,0:T(8,128)(2,1)} %all-gather.16.cloned.1.call-done, f32[512,768]{1,0:T(8,128)} %copy-done.13, f32[768]{0:T(1024)S(1)} %get-tuple-element.371, ...), kind=kOutput, calls=%fused_computation.222 | convolution fusion | flops 2521693696 | bytes 25190400 | tf_op jit(solution)/shard_map/dot_general | solution.py:155
  492.7 8.9 copy.99
  513.7 11.4 convert_reduce_fusion
  539.4 251.5 %while.31 = (s32[]{:T(128)}, f32[512,12,64]{0,2,1:T(8,128)}, bf16[8,512,12,64]{1,3,2,0:T(8,128)(2,1)}, bf16[8,512,12,64]{1,3,2,0:T(8,128)(2,1)}, bf16[8,512,12,6...) while((s32[]{:T(128)}, f32[512,12,64]{0,2,1:T(8,128)}, ...), condition=%wide.region_24.25_spmd.clone, body=%wide.region_23.24_spmd.clone.sunk | while | flops 2047082496 | bytes 195125520 | solution.py:254
  547.5 8.4 fusion.165
  578.5 8.4 fusion.165
  609.9 8.4 fusion.165
  641.2 8.4 fusion.165
  672.6 8.4 fusion.165
  704.1 8.4 fusion.165
  735.5 8.4 fusion.165
  766.9 8.4 fusion.165
  842.0 24.1 %reduce-scatter.14.cloned.1.call-done = bf16[512,768]{0,1:T(8,128)(2,1)} async-done(((bf16[4096,768]{0,1:T(8,128)(2,1)}), bf16[512,768]{0,1:T(8,128)(2,1)}) %reduce-scatter.14.cloned.1.call-update) | async-done | bytes 786448 | tf_op jit(solution)/shard_map/reduce_scatter | solution.py:270
  866.1 65.5 %reduce-scatter.12.cloned.1.call-done = bf16[512,768]{0,1:T(8,128)(2,1)} async-done(((bf16[4096,768]{0,1:T(8,128)(2,1)}), bf16[512,768]{0,1:T(8,128)(2,1)}) %reduce-scatter.12.cloned.1.call-update) | async-done | bytes 786448 | tf_op jit(solution)/shard_map/reduce_scatter | solution.py:267
  946.5 87.5 %reduce-scatter.24.cloned.1.call-done = f32[96,2]{1,0:T(8,128)} async-done(((f32[3072,2]{1,0:T(8,128)}), f32[96,2]{1,0:T(8,128)}) %reduce-scatter.24.cloned.1.call-update) | async-done | bytes 784
  1043.7 40.8 %all-reduce.3 = (f32[3,768]{1,0:T(4,128)S(1)}, f32[7,768]{1,0:T(8,128)S(1)}, f32[3072]{0:T(1024)S(1)}) all-reduce(f32[3,768]{1,0:T(4,128)S(1)} %pad_maximum_fusion.2, f32[7,768]{1,0:T(8,128)S(1)} %stack.36, f32[3072]{0:T(1024)S(1)} %copy-done.31), channel_id=8, replica_groups=mesh['ctx'=8,'fsdp'=4] {'ctx','fsdp'}, use_global_device_ids=true, to_apply=%region_36.37.clone | all-reduce | flops 10752 | bytes 86016
  1086.5 51.3 %reduce-scatter.18.cloned.1.call-done = f32[24,768]{1,0:T(8,128)} async-done(((f32[768,768]{1,0:T(8,128)}), f32[24,768]{1,0:T(8,128)}) %reduce-scatter.18.cloned.1.call-update) | async-done | bytes 73744 | tf_op jit(solution)/shard_map/reduce_scatter | solution.py:300
  1137.7 142.2 %reduce-scatter.20.cloned.1.call-done = f32[24,3072]{1,0:T(8,128)} async-done(((f32[768,3072]{1,0:T(8,128)}), f32[24,3072]{1,0:T(8,128)}) %reduce-scatter.20.cloned.1.call-update) | async-done | bytes 294928 | tf_op jit(solution)/shard_map/reduce_scatter | solution.py:301
  1279.9 140.8 %reduce-scatter.22.cloned.1.call-done = f32[96,768]{1,0:T(8,128)} async-done(((f32[3072,768]{1,0:T(8,128)}), f32[96,768]{1,0:T(8,128)}) %reduce-scatter.22.cloned.1.call-update) | async-done | bytes 294928 | tf_op jit(solution)/shard_map/reduce_scatter | solution.py:302
  1420.8 125.3 %reduce-scatter.16.cloned.1.call-done = f32[24,2304]{1,0:T(8,128)} async-done(((f32[768,2304]{1,0:T(8,128)}), f32[24,2304]{1,0:T(8,128)}) %reduce-scatter.16.cloned.1.call-update) | async-done | bytes 221200 | tf_op jit(solution)/shard_map/reduce_scatter | solution.py:299
  (438 shorter events, 429.7 us)
Async XLA Ops:
  7.2 75.3 %all-gather.10.cloned.1.call-start = ((), (), s32[]{:S(2)}) async-start(), calls=%async_computation.7 | async-start | bytes 4423680 | tf_op jit(solution)/shard_map/all_gather | solution.py:82
  7.9 244.3 %all-gather.12.cloned.1.call-start = ((), (), s32[]{:S(2)}) async-start(), calls=%async_computation.8 | async-start | bytes 7077888 | tf_op jit(solution)/shard_map/all_gather | solution.py:110
  35.4 51.5 %copy-start.32 = (f32[768]{0:T(1024)}, f32[768]{0:T(1024)S(1)}, u32[]{:S(2)}) copy-start(f32[768]{0:T(1024)S(1)} %get-tuple-element.379) | copy-start | bytes 9220
  36.0 50.9 %copy-start.45 = (f32[768]{0:T(1024)}, f32[768]{0:T(1024)S(1)}, u32[]{:S(2)}) copy-start(f32[768]{0:T(1024)S(1)} %get-tuple-element.376) | copy-start | bytes 9220
  36.0 420.1 %copy-start.49 = (f32[768]{0:T(1024)}, f32[768]{0:T(1024)S(1)}, u32[]{:S(2)}) copy-start(f32[768]{0:T(1024)S(1)} %get-tuple-element.373) | copy-start | bytes 9220
  36.0 424.4 %copy-start.47 = (f32[768]{0:T(1024)}, f32[768]{0:T(1024)S(1)}, u32[]{:S(2)}) copy-start(f32[768]{0:T(1024)S(1)} %get-tuple-element.371) | copy-start | bytes 9220
  37.3 49.5 %copy-start.34 = (f32[512]{0:T(512)}, f32[512]{0:T(512)S(1)}, u32[]{:S(2)}) copy-start(f32[512]{0:T(512)S(1)} %broadcast_multiply_fusion.4) | copy-start | bytes 6148
  38.8 48.0 %copy-start.38 = (f32[512]{0:T(512)}, f32[512]{0:T(512)S(1)}, u32[]{:S(2)}) copy-start(f32[512]{0:T(512)S(1)} %fusion.57) | copy-start | bytes 6148
  38.8 48.0 %copy-start.36 = (f32[512]{0:T(512)}, f32[512]{0:T(512)S(1)}, u32[]{:S(2)}) copy-start(f32[512]{0:T(512)S(1)} %fusion.83) | copy-start | bytes 6148
  89.1 76.7 %copy-start.59 = (s32[1,4]{1,0:T(1,128)S(1)}, s32[1,4]{1,0:T(1,128)}, u32[]{:S(2)}) copy-start(s32[1,4]{1,0:T(1,128)} %param.18) | copy-start | bytes 52
  89.1 76.8 %copy-start.56 = (s32[1,16]{1,0:T(1,128)S(1)}, s32[1,16]{1,0:T(1,128)}, u32[]{:S(2)}) copy-start(s32[1,16]{1,0:T(1,128)} %param.19) | copy-start | bytes 196
  89.1 89.4 %copy-start.57 = (bf16[768]{0:T(1024)(128)(2,1)S(1)}, bf16[768]{0:T(1024)(128)(2,1)}, u32[]{:S(2)}) copy-start(bf16[768]{0:T(1024)(128)(2,1)} %param.26) | copy-start | bytes 4612
  89.1 103.2 %copy-start.55 = (bf16[2,768]{1,0:T(2,128)(2,1)S(1)}, bf16[2,768]{1,0:T(2,128)(2,1)}, u32[]{:S(2)}) copy-start(bf16[2,768]{1,0:T(2,128)(2,1)} %param.27) | copy-start | bytes 9220
  90.1 366.0 %all-gather.14.cloned.1.call-start = ((), (), s32[]{:S(2)}) async-start(), calls=%async_computation.9 | async-start | bytes 1474560 | tf_op jit(solution)/shard_map/all_gather | solution.py:83
  90.8 369.5 %all-gather.16.cloned.1.call-start = ((), (), s32[]{:S(2)}) async-start(), calls=%async_computation.10 | async-start | bytes 5898240 | tf_op jit(solution)/shard_map/all_gather | solution.py:84
  91.4 390.6 %all-gather.18.cloned.1.call-start = ((), (), s32[]{:S(2)}) async-start(), calls=%async_computation.11 | async-start | bytes 5898240 | tf_op jit(solution)/shard_map/all_gather | solution.py:85
  92.0 400.7 %all-gather.20.cloned.1.call-start = ((), (), s32[]{:S(2)}) async-start(), calls=%async_computation.12 | async-start | bytes 7077888 | tf_op jit(solution)/shard_map/all_gather | solution.py:242
  94.2 113.6 %copy-start.9 = (bf16[512,768]{1,0:T(8,128)(2,1)}, bf16[512,768]{1,0:T(8,128)(2,1)S(1)}, u32[]{:S(2)}) copy-start(bf16[512,768]{1,0:T(8,128)(2,1)S(1)} %get-tuple-element.455) | copy-start | bytes 2359300
  94.2 20.8 %collective-permute-start = (bf16[512,768]{1,0:T(8,128)(2,1)S(1)}, bf16[512,768]{1,0:T(8,128)(2,1)S(1)}, u32[]{:S(2)}, u32[]{:S(2)}) collective-permute-start(bf16[512,768]{1,0:T(8,128)(2,1)S(1)} %get-tuple-element.455), channel_id=1, source_target_pairs={{0,4},{4,8},{8,12},{12,16},{16,20},{20,24},{24,28},{28,0},{1,5},{5... | collective-permute-start | bytes 2359304 | tf_op jit(solution)/shard_map/ppermute | solution.py:113
  115.0 26.0 %collective-permute-start.1 = (bf16[512,768]{1,0:T(8,128)(2,1)S(1)}, bf16[512,768]{1,0:T(8,128)(2,1)S(1)}, u32[]{:S(2)}, u32[]{:S(2)}) collective-permute-start(bf16[512,768]{1,0:T(8,128)(2,1)S(1)} %collective-permute-done), channel_id=1, source_target_pairs={{0,4},{4,8},{8,12},{12,16},{16,20},{20,24},{24,28},{28,0},{1,5},{5... | collective-permute-start | bytes 2359304 | tf_op jit(solution)/shard_map/ppermute | solution.py:113
  141.0 12.3 collective-permute-start.2
  153.3 12.4 copy-start.22
  153.3 12.4 collective-permute-start.3
  165.7 12.6 collective-permute-start.4
  178.3 27.5 %collective-permute-start.5 = (bf16[512,768]{1,0:T(8,128)(2,1)}, bf16[512,768]{1,0:T(8,128)(2,1)}, u32[]{:S(2)}, u32[]{:S(2)}) collective-permute-start(bf16[512,768]{1,0:T(8,128)(2,1)} %collective-permute-done.4), channel_id=1, source_target_pairs={{0,4},{4,8},{8,12},{12,16},{16,20},{20,24},{24,28},{28,0},{1,5},{5... | collective-permute-start | bytes 2359304 | tf_op jit(solution)/shard_map/ppermute | solution.py:113
  205.8 12.7 collective-permute-start.6
  207.8 15.5 copy-start.23
  207.8 15.7 %copy-start.10 = (bf16[512,768]{1,0:T(8,128)(2,1)S(1)}, bf16[512,768]{1,0:T(8,128)(2,1)}, u32[]{:S(2)}) copy-start(bf16[512,768]{1,0:T(8,128)(2,1)} %copy-done.9) | copy-start | bytes 2359300
  207.8 658.3 %reduce-scatter.14.cloned.1.call-start = ((), (), s32[]{:S(2)}) async-start(), calls=%async_computation.14 | async-start | bytes 7077888 | tf_op jit(solution)/shard_map/reduce_scatter | solution.py:270
  460.4 21.6 %copy-start.24 = (bf16[1,512,768]{2,1,0:T(8,128)(2,1)S(1)}, bf16[1,512,768]{2,1,0:T(8,128)(2,1)}, u32[]{:S(2)}) copy-start(bf16[1,512,768]{2,1,0:T(8,128)(2,1)} %param.17) | copy-start | bytes 2359300
  460.4 21.6 %copy-start.29 = (f32[4,1,768]{2,1,0:T(1,128)S(1)}, f32[4,1,768]{2,1,0:T(1,128)}, u32[]{:S(2)}) copy-start(f32[4,1,768]{2,1,0:T(1,128)} %convert_element_type.127) | copy-start | bytes 36868
  501.6 12.1 slice-start
  513.7 11.4 copy-start.14
  649.7 10.7 copy-start.3
  681.1 10.7 copy-start.3
  712.5 10.7 copy-start.3
  743.9 10.7 copy-start.3
  804.8 126.9 %reduce-scatter.12.cloned.1.call-start = ((), (), s32[]{:S(2)}) async-start(), calls=%async_computation.13 | async-start | bytes 7077888 | tf_op jit(solution)/shard_map/reduce_scatter | solution.py:267
  819.0 215.0 %reduce-scatter.24.cloned.1.call-start = ((), (), s32[]{:S(2)}) async-start(), calls=%async_computation.19 | async-start | bytes 1622016
  821.4 316.4 %reduce-scatter.18.cloned.1.call-start = ((), (), s32[]{:S(2)}) async-start(), calls=%async_computation.16 | async-start | bytes 2433024 | tf_op jit(solution)/shard_map/reduce_scatter | solution.py:300
  825.0 454.9 %reduce-scatter.20.cloned.1.call-start = ((), (), s32[]{:S(2)}) async-start(), calls=%async_computation.17 | async-start | bytes 9732096 | tf_op jit(solution)/shard_map/reduce_scatter | solution.py:301
  832.3 588.4 %reduce-scatter.22.cloned.1.call-start = ((), (), s32[]{:S(2)}) async-start(), calls=%async_computation.18 | async-start | bytes 9732096 | tf_op jit(solution)/shard_map/reduce_scatter | solution.py:302
  840.4 91.2 %copy-start.12 = (bf16[1,512,768]{2,1,0:T(8,128)(2,1)S(1)}, bf16[1,512,768]{2,1,0:T(8,128)(2,1)}, u32[]{:S(2)}) copy-start(bf16[1,512,768]{2,1,0:T(8,128)(2,1)} %param.16) | copy-start | bytes 2359300
  840.4 91.2 %copy-start.33 = (f32[768]{0:T(1024)S(1)}, f32[768]{0:T(1024)}, u32[]{:S(2)}) copy-start(f32[768]{0:T(1024)} %copy-done.32) | copy-start | bytes 9220
  840.4 91.2 %copy-start.35 = (f32[512]{0:T(512)S(1)}, f32[512]{0:T(512)}, u32[]{:S(2)}) copy-start(f32[512]{0:T(512)} %copy-done.34) | copy-start | bytes 6148
  840.4 91.2 %copy-start.37 = (f32[512]{0:T(512)S(1)}, f32[512]{0:T(512)}, u32[]{:S(2)}) copy-start(f32[512]{0:T(512)} %copy-done.36) | copy-start | bytes 6148
  840.5 91.2 %copy-start.46 = (f32[768]{0:T(1024)S(1)}, f32[768]{0:T(1024)}, u32[]{:S(2)}) copy-start(f32[768]{0:T(1024)} %copy-done.45) | copy-start | bytes 9220
  840.5 705.6 %reduce-scatter.16.cloned.1.call-start = ((), (), s32[]{:S(2)}) async-start(), calls=%async_computation.15 | async-start | bytes 7299072 | tf_op jit(solution)/shard_map/reduce_scatter | solution.py:299
  (62 other events, 307.0 us)
Sparse Core Ops, SparseCore 0:
  9.6 72.8 all-gather.9
  90.2 55.7 all-gather.11
  147.6 29.3 all-gather.13
  178.4 88.6 all-gather.15
  268.5 87.8 all-gather.17
  358.2 43.9 all-gather.19
  804.9 61.1 reduce-scatter.13
  869.9 61.7 reduce-scatter.11
  936.9 97.0 reduce-scatter.23
  1039.7 98.0 reduce-scatter.17
  1145.2 134.6 reduce-scatter.19
  1286.3 134.4 reduce-scatter.21
  1428.0 118.0 reduce-scatter.15
